TPU v7x, 32 devices: a whole 2x2x4 slice. The times are simulated.
32 devices in a mesh: dp: 16 (over z, y, x), mp: 2 (over core).
Axes of the slice: x: 2, y: 2, z: 4, core: 2. Of those that a mesh axis runs over, the one named last changes fastest.
Arguments:
- tokens: bfloat16 [512, 7168], P('dp', 'mp'), may hold values from -6 to 6
- gate_weight: bfloat16 [7168, 18432], P('mp', 'dp'), may hold values from -0.0625 to 0.0625
- up_weight: bfloat16 [7168, 18432], P('mp', 'dp'), may hold values from -0.0625 to 0.0625
- down_weight: bfloat16 [18432, 7168], P('dp', 'mp'), may hold values from -0.046875 to 0.046875
- gate_round: bfloat16 [7168, 18432], P('mp', 'dp'), may hold values from -8 to 8
- up_round: bfloat16 [7168, 18432], P('mp', 'dp'), may hold values from -8 to 8
- down_round: bfloat16 [18432, 7168], P('dp', 'mp'), may hold values from -8 to 8
- quant_scale: float32 [2, 18432], P(None, 'dp'), may hold values from 0.3 to 3
- quant_bits: int32 [2, 18432], P(None, 'dp'), may hold values from 2 to 4
- quant_zero: int32 [2, 18432], P(None, 'dp'), may hold values from 0 to 2
- down_scale: float32 [7168], P('mp'), may hold values from 0.3 to 3
- down_bits: int32 [7168], P('mp'), may hold values from 2 to 4
- down_zero: int32 [7168], P('mp'), may hold values from 0 to 2
- fisher: float32 [512], replicated, may hold values from 1 to 300, as said below
Outputs:
- loss_value: float32 [], replicated
- grad_gate: bfloat16 [7168, 18432], P('mp', 'dp')
- grad_up: bfloat16 [7168, 18432], P('mp', 'dp')
- grad_down: bfloat16 [18432, 7168], P('dp', 'mp')
Inputs may be any that keep to these rules, and one draw needn't show every extreme that they name: `fisher`: positive weights.
All inputs are finite; a program needn't handle non-finite values.
Results may differ from a plain program's by a relative error of at most 0.0059.
Values may be sent and summed in bfloat16 or wider, within the bound.
A program may use at most 192 MiB of HBM per device.

v0:
```python
import jax
import jax.numpy as jnp
from jax import lax
from jax.sharding import PartitionSpec as P

D = 7168
FF = 18432


def soft_weight(weight, variable, channel_scale, bit_width, zero_point, fan_in):
    quant_step = channel_scale / jnp.sqrt(jnp.float32(fan_in))
    offset = jnp.clip(1.2 * jax.nn.sigmoid(variable.astype(jnp.float32)) - 0.1, 0.0, 1.0)
    ceiling = (jnp.left_shift(jnp.int32(1), bit_width) - 1).astype(jnp.float32)
    zero_level = zero_point.astype(jnp.float32)
    levels = jnp.clip(
        weight.astype(jnp.float32) / quant_step + offset - 0.5 + zero_level, 0.0, ceiling
    )
    return (quant_step * (levels - zero_level)).astype(jnp.bfloat16)


def contract_rows(left, right):
    return lax.dot_general(
        left, right, (((0,), (0,)), ((), ())), preferred_element_type=jnp.float32
    )


def shards(
    tokens,
    gate_weight,
    up_weight,
    down_weight,
    gate_round,
    up_round,
    down_round,
    quant_scale,
    quant_bits,
    quant_zero,
    down_scale,
    down_bits,
    down_zero,
    fisher,
):
    own_rows = tokens.shape[0]
    hidden_cols = gate_weight.shape[1]
    all_tokens = lax.all_gather(tokens, "dp", axis=0, tiled=True)
    total_rows = all_tokens.shape[0]
    gate_student = soft_weight(
        gate_weight, gate_round, quant_scale[0], quant_bits[0], quant_zero[0], D
    )
    up_student = soft_weight(up_weight, up_round, quant_scale[1], quant_bits[1], quant_zero[1], D)
    stacked = jnp.concatenate([gate_weight, up_weight, gate_student, up_student], axis=1)
    partial_value = jnp.dot(all_tokens, stacked, preferred_element_type=jnp.float32)
    shares = lax.psum_scatter(partial_value, "mp", scatter_dimension=0, tiled=True)
    gate_teacher = shares[:, :hidden_cols]
    up_teacher = shares[:, hidden_cols : 2 * hidden_cols]
    gate_own = shares[:, 2 * hidden_cols : 3 * hidden_cols]
    up_own = shares[:, 3 * hidden_cols :]
    hidden_teacher = (jax.nn.silu(gate_teacher) * up_teacher).astype(jnp.bfloat16)
    hidden_student = (jax.nn.silu(gate_own) * up_own).astype(jnp.bfloat16)
    hidden = lax.all_gather(
        jnp.concatenate([hidden_teacher, hidden_student], axis=1), "mp", axis=0, tiled=True
    )
    down_student = soft_weight(down_weight, down_round, down_scale, down_bits, down_zero, FF)
    terms = jnp.dot(
        hidden,
        jnp.concatenate([-down_weight, down_student], axis=0),
        preferred_element_type=jnp.float32,
    )
    summed = lax.psum_scatter(terms, "dp", scatter_dimension=0, tiled=True)
    token_weight = lax.dynamic_slice_in_dim(fisher, lax.axis_index("dp") * own_rows, own_rows)
    weighted = token_weight[:, None] * summed
    partial_loss = jnp.sum(weighted * summed)
    local_grad = (2.0 * weighted).astype(jnp.bfloat16)
    loss_sum = lax.psum(partial_loss, ("dp", "mp"))
    out_grad = lax.all_gather(local_grad, "dp", axis=0, tiled=True)
    loss_value = loss_sum / (total_rows * D)
    grad_down = contract_rows(hidden[:, hidden_cols:], out_grad).astype(jnp.bfloat16)
    hidden_part = lax.dot_general(
        out_grad, down_student, (((1,), (1,)), ((), ())), preferred_element_type=jnp.float32
    )
    hidden_grad = lax.psum_scatter(hidden_part, "mp", scatter_dimension=0, tiled=True)
    sigmoid_gate = jax.nn.sigmoid(gate_own)
    gate_grad = (
        hidden_grad * up_own * sigmoid_gate * (1.0 + gate_own * (1.0 - sigmoid_gate))
    ).astype(jnp.bfloat16)
    up_grad = (hidden_grad * gate_own * sigmoid_gate).astype(jnp.bfloat16)
    both_grads = lax.all_gather(
        jnp.concatenate([gate_grad, up_grad], axis=1), "mp", axis=0, tiled=True
    )
    weight_grads = contract_rows(all_tokens, both_grads)
    grad_gate = weight_grads[:, :hidden_cols].astype(jnp.bfloat16)
    grad_up = weight_grads[:, hidden_cols:].astype(jnp.bfloat16)
    return (loss_value, grad_gate, grad_up, grad_down)


def solution(mesh):
    in_specs = (
        P("dp", "mp"),
        P("mp", "dp"),
        P("mp", "dp"),
        P("dp", "mp"),
        P("mp", "dp"),
        P("mp", "dp"),
        P("dp", "mp"),
        P(None, "dp"),
        P(None, "dp"),
        P(None, "dp"),
        P("mp"),
        P("mp"),
        P("mp"),
        P(),
    )
    out_specs = (P(), P("mp", "dp"), P("mp", "dp"), P("dp", "mp"))
    return jax.shard_map(shards, mesh=mesh, in_specs=in_specs, out_specs=out_specs, check_vma=False)
```

profile of v0, /device:TPU:0, one launch (start us, length us, event | category | flops | bytes accessed | tf_op | source)
XLA Modules:
  0.0 532.8 jit_solution(1226961479305919175)
XLA Ops:
  7.2 0.0 all-gather.5.cloned.1.call-start
  7.2 0.7 all-gather.5.cloned.1.call-update
  7.9 0.0 reduce-scatter.4.cloned.1.call-start
  7.9 0.8 convert_reduce_fusion.2
  8.8 0.8 convert_reduce_fusion.3
  9.6 0.8 multiply_reduce_fusion.1
  10.4 24.4 %multiply_convert_fusion.1 = (bf16[3584,1152]{1,0:T(8,128)(2,1)}, bf16[3584,1152]{1,0:T(8,128)(2,1)}) fusion(bf16[3584,1152]{1,0:T(8,128)(2,1)} %param.19, bf16[3584,1152]{1,0:T(8,128)(2,1)} %param.16, f32[1152]{0:T(1024)S(1)} %get-tuple-element.13, f32[1152]{0:T(1024)S(1)} %get-tuple-element.11, f32[1152]{0:T(1024)S(1)} %get-tuple-element.9, ...), kind=kLoop, calls=%fused_computation.15 | loop fusion | flops 140378112 | bytes 49572864 | tf_op jit(solution)/shard_map/convert_element_type | solution.py:18
  34.7 50.4 %all-gather.5.cloned.1.call-done = bf16[512,3584]{1,0:T(8,128)(2,1)} async-done(((bf16[32,3584]{1,0:T(8,128)(2,1)}), bf16[512,3584]{1,0:T(8,128)(2,1)}) %all-gather.5.cloned.1.call-update) | async-done | bytes 3670032 | tf_op jit(solution)/shard_map/all_gather | solution.py:45
  85.1 25.0 %fusion.13 = f32[512,4608]{0,1:T(8,128)} fusion(bf16[512,3584]{1,0:T(8,128)(2,1)} %all-gather.5.cloned.1.call-done, bf16[3584,1152]{1,0:T(8,128)(2,1)} %get-tuple-element.22, bf16[3584,1152]{1,0:T(8,128)(2,1)} %get-tuple-element.23, bf16[3584,1152]{1,0:T(8,128)(2,1)} %param.16, bf16[3584,1152]{1,0:T(8,128)(2,1)} %param.15), kind=kOutput, calls=%fused_computation.18 | convolution fusion | flops 17043554304 | bytes 46137344 | tf_op jit(solution)/shard_map/dot_general | solution.py:52
  110.1 0.0 copy-start
  110.1 0.0 copy-start.1
  110.1 0.0 copy-start.2
  110.1 0.0 reduce-scatter.4.cloned.1.call-update
  110.1 0.0 all-gather.7.cloned.1.call-start
  110.2 0.6 copy-done
  110.8 0.0 copy-done.1
  110.9 0.0 copy-done.2
  110.9 15.0 %reduce-scatter.4.cloned.1.call-done = f32[256,4608]{0,1:T(8,128)} async-done(((f32[512,4608]{0,1:T(8,128)}), f32[256,4608]{0,1:T(8,128)}) %reduce-scatter.4.cloned.1.call-update) | async-done | bytes 4718608 | tf_op jit(solution)/shard_map/reduce_scatter | solution.py:53
  125.9 3.0 fusion.17
  128.9 1.1 pad_maximum_fusion
  130.0 0.0 all-gather.7.cloned.1.call-update
  130.0 0.2 reduce-scatter.6.cloned.1.call-start
  130.2 14.3 %multiply_convert_fusion = bf16[1152,3584]{1,0:T(8,128)(2,1)} fusion(bf16[1152,3584]{1,0:T(8,128)(2,1)} %param.20, bf16[1152,3584]{1,0:T(8,128)(2,1)} %param.17, f32[3584]{0:T(1024)S(1)} %convert_element_type.84, f32[3584]{0:T(1024)S(1)} %add_convert_fusion, f32[3584]{0:T(1024)S(1)} %broadcast_multiply_fusion), kind=kLoop, calls=%fused_computation.14 | loop fusion | flops 70189056 | bytes 24815616 | tf_op jit(solution)/shard_map/convert_element_type | solution.py:18
  144.5 8.2 %neg.24 = bf16[1152,3584]{1,0:T(8,128)(2,1)} negate(bf16[1152,3584]{1,0:T(8,128)(2,1)} %param.17) | non-fusion elementwise | flops 4128768 | bytes 16515072 | tf_op jit(solution)/shard_map/neg | solution.py:66
  152.7 0.0 all-gather.7.cloned.1.call-done
  152.7 15.0 %fusion.9 = f32[512,3584]{1,0:T(8,128)} fusion(bf16[512,2304]{0,1:T(8,128)(2,1)} %all-gather.7.cloned.1.call-done, bf16[1152,3584]{1,0:T(8,128)(2,1)} %multiply_convert_fusion, bf16[1152,3584]{1,0:T(8,128)(2,1)} %neg.24), kind=kOutput, calls=%fused_computation.10 | convolution fusion | flops 8488747008 | bytes 26214400 | tf_op jit(solution)/shard_map/dot_general | solution.py:64
  167.7 0.0 reduce-scatter.6.cloned.1.call-update
  167.7 0.0 all-gather.9.cloned.1.call-start
  167.8 0.8 dynamic_slice.3
  168.5 157.4 %reduce-scatter.6.cloned.1.call-done = f32[32,3584]{1,0:T(8,128)} async-done(((f32[512,3584]{1,0:T(8,128)}), f32[32,3584]{1,0:T(8,128)}) %reduce-scatter.6.cloned.1.call-update) | async-done | bytes 458768 | tf_op jit(solution)/shard_map/reduce_scatter | solution.py:69
  326.0 2.4 fusion.19
  328.4 0.0 all-gather.9.cloned.1.call-update
  328.4 0.0 reduce-scatter.8.cloned.1.call-start
  328.5 74.7 %all-gather.9.cloned.1.call-done = bf16[512,3584]{1,0:T(8,128)(2,1)} async-done(((bf16[32,3584]{1,0:T(8,128)(2,1)}), bf16[512,3584]{1,0:T(8,128)(2,1)}) %all-gather.9.cloned.1.call-update) | async-done | bytes 3670032 | tf_op jit(solution)/shard_map/all_gather | solution.py:75
  403.2 10.3 %fusion.23 = f32[512,1152]{0,1:T(8,128)} fusion(bf16[512,3584]{1,0:T(8,128)(2,1)} %all-gather.9.cloned.1.call-done, bf16[1152,3584]{1,0:T(8,128)(2,1)} %multiply_convert_fusion), kind=kOutput, calls=%fused_computation.43 | convolution fusion | flops 4227858432 | bytes 14286848 | tf_op jit(solution)/shard_map/dot_general | solution.py:78
  413.5 0.0 reduce-scatter.8.cloned.1.call-update
  413.6 0.3 all-gather.11.cloned.1.call-start
  413.8 8.4 %reduce-scatter.8.cloned.1.call-done = f32[256,1152]{0,1:T(8,128)} async-done(((f32[512,1152]{0,1:T(8,128)}), f32[256,1152]{0,1:T(8,128)}) %reduce-scatter.8.cloned.1.call-update) | async-done | bytes 1179664 | tf_op jit(solution)/shard_map/reduce_scatter | solution.py:81
  422.2 2.5 multiply_convert_fusion.4
  424.7 1.1 pad_maximum_fusion.1
  425.8 0.0 all-gather.11.cloned.1.call-update
  425.8 40.9 %psum.7 = f32[]{:T(128)} all-reduce(f32[]{:T(128)} %get-tuple-element.21), channel_id=1, replica_groups=mesh['dp'=16,'mp'=2] {'dp','mp'}, use_global_device_ids=true, to_apply=%region_3.4 | all-reduce | flops 1 | bytes 8 | tf_op jit(solution)/shard_map/psum | solution.py:74
  467.3 0.0 copy-done.3
  467.3 8.7 %convolution_convert_fusion.1 = bf16[1152,3584]{1,0:T(8,128)(2,1)} fusion(bf16[512,3584]{1,0:T(8,128)(2,1)} %all-gather.9.cloned.1.call-done, bf16[512,2304]{0,1:T(8,128)(2,1)S(1)} %copy-done.3), kind=kOutput, calls=%fused_computation.17 | convolution fusion | flops 4231987200 | bytes 13107200 | tf_op jit(solution)/shard_map/dot_general | solution.py:22
  476.0 14.4 %fusion.8 = bf16[3584,2304]{0,1:T(8,128)(2,1)} fusion(bf16[512,2304]{0,1:T(8,128)(2,1)} %all-gather.11.cloned.1.call-done, bf16[512,3584]{1,0:T(8,128)(2,1)} %all-gather.5.cloned.1.call-done), kind=kOutput, calls=%fused_computation.9 | convolution fusion | flops 8463974400 | bytes 22544384 | tf_op jit(solution)/shard_map/dot_general | solution.py:22
  490.4 11.4 %fusion.22 = (bf16[3584,1152]{0,1:T(8,128)(2,1)}, bf16[3584,1152]{0,1:T(8,128)(2,1)}) fusion(bf16[3584,2304]{0,1:T(8,128)(2,1)} %fusion.8), kind=kLoop, calls=%fused_computation.42 | loop fusion | bytes 33030144 | tf_op jit(solution)/shard_map/slice | solution.py:92
  501.8 11.5 %copy.19 = bf16[3584,1152]{1,0:T(8,128)(2,1)} copy(bf16[3584,1152]{0,1:T(8,128)(2,1)} %get-tuple-element.15) | data formatting | bytes 16515072
  513.3 11.5 %copy.20 = bf16[3584,1152]{1,0:T(8,128)(2,1)} copy(bf16[3584,1152]{0,1:T(8,128)(2,1)} %get-tuple-element.14) | data formatting | bytes 16515072
  (5 shorter events, 0.0 us)
Async XLA Ops:
  7.2 77.9 %all-gather.5.cloned.1.call-start = ((), (), s32[]{:S(2)}) async-start(), calls=%async_computation.3 | async-start | bytes 3899392 | tf_op jit(solution)/shard_map/all_gather | solution.py:45
  7.9 118.0 %reduce-scatter.4.cloned.1.call-start = ((), (), s32[]{:S(2)}) async-start(), calls=%async_computation.4 | async-start | bytes 14155776 | tf_op jit(solution)/shard_map/reduce_scatter | solution.py:53
  110.1 0.7 copy-start
  110.1 0.7 copy-start.1
  110.1 0.7 copy-start.2
  110.1 42.5 %all-gather.7.cloned.1.call-start = ((), (), s32[]{:S(2)}) async-start(), calls=%async_computation.5 | async-start | bytes 3538944 | tf_op jit(solution)/shard_map/all_gather | solution.py:60
  130.0 196.0 %reduce-scatter.6.cloned.1.call-start = ((), (), s32[]{:S(2)}) async-start(), calls=%async_computation.6 | async-start | bytes 7798784 | tf_op jit(solution)/shard_map/reduce_scatter | solution.py:69
  167.7 235.5 %all-gather.9.cloned.1.call-start = ((), (), s32[]{:S(2)}) async-start(), calls=%async_computation.7 | async-start | bytes 3899392 | tf_op jit(solution)/shard_map/all_gather | solution.py:75
  328.4 93.8 %reduce-scatter.8.cloned.1.call-start = ((), (), s32[]{:S(2)}) async-start(), calls=%async_computation.8 | async-start | bytes 3538944 | tf_op jit(solution)/shard_map/reduce_scatter | solution.py:81
  413.5 53.8 %copy-start.3 = (bf16[512,2304]{0,1:T(8,128)(2,1)S(1)}, bf16[512,2304]{0,1:T(8,128)(2,1)}, u32[]{:S(2)}) copy-start(bf16[512,2304]{0,1:T(8,128)(2,1)} %all-gather.7.cloned.1.call-done) | copy-start | bytes 7077892
  413.6 62.5 %all-gather.11.cloned.1.call-start = ((), (), s32[]{:S(2)}) async-start(), calls=%async_computation.9 | async-start | bytes 3538944 | tf_op jit(solution)/shard_map/all_gather | solution.py:87
Sparse Core Ops, SparseCore 0:
  10.7 74.3 all-gather.4
  110.3 15.5 reduce-scatter.3
  130.1 11.7 all-gather.6
  167.8 158.0 reduce-scatter.5
  329.1 73.9 all-gather.8
  413.7 8.4 reduce-scatter.7
  426.0 11.7 all-gather.10
where the time goes:
time: 534 us; the launch traced here: 533 us
  waiting for transfers between devices  307 us (57%)
  matrix products  73.5 us (14%)
  other arithmetic  59.4 us (11%)
  blocking collectives  40.9 us (8%)
  local copies, waits for them, and re-layouts  35.8 us (7%)
  between operations  16 us (3%)
    reduce_scatter x1, waiting for transfers between devices, shards(): summed = lax.psum_scatter(terms, 'dp', scatter_dimension=0, tiled=True)  157 us
    all_gather x1, waiting for transfers between devices, shards(): out_grad = lax.all_gather(local_grad, 'dp', axis=0, tiled=True)  74.7 us
    all_gather x1, waiting for transfers between devices, shards(): all_tokens = lax.all_gather(tokens, 'dp', axis=0, tiled=True)  50.4 us
    psum x1, blocking collectives, shards(): loss_sum = lax.psum(partial_loss, ('dp', 'mp'))  40.9 us
    convert_element_type x2, other arithmetic, soft_weight(): return (quant_step * (levels - zero_level)).astype(jnp.bfloat16)  38.6 us
    dot_general x1, matrix products, shards(): jnp.dot(all_tokens, stacked, preferred_element_type=jnp.float32)  25 us
    unnamed x10, local copies, waits for them, and re-layouts  23.7 us
    dot_general x2, matrix products, contract_rows(): lax.dot_general(left, right, (((0,), (0,)), ((), ())), preferred_element_...  23.1 us
  transfers between devices with their start and end apart: 7, of which 5 were waited for; matrix products, arithmetic and copies ran while one was open for 11% of the time, Pallas kernels for 0%

commit v1 on v0

--- a/solution.py
+++ b/solution.py
@@ -1,10 +1,243 @@
+import functools
+
 import jax
 import jax.numpy as jnp
 from jax import lax
+from jax.experimental import pallas as pl
+from jax.experimental.pallas import tpu as pltpu
 from jax.sharding import PartitionSpec as P
 
 D = 7168
 FF = 18432
+MESH = pl.DeviceIdType.MESH
+LANES = 128
+
+
+def ring_index(position, count):
+    if count % 4:
+        return position
+    depth = count // 4
+    column, run = position // depth, position % depth
+    level = run + (column % 2) * (depth - 1 - 2 * run)
+    return level * 4 + column + (column // 2) * (5 - 2 * column)
+
+
+def ring_position(index, count):
+    if count % 4:
+        return index
+    depth = count // 4
+    level, corner = index // 4, index % 4
+    column = corner + (corner // 2) * (5 - 2 * corner)
+    return column * depth + level + (column % 2) * (depth - 1 - 2 * level)
+
+
+def column_pieces(columns, parts=4):
+    tiles = columns // LANES
+    edges = [tiles * k // parts * LANES for k in range(parts)] + [columns]
+    return [(lo, hi) for lo, hi in zip(edges[:-1], edges[1:]) if hi > lo]
+
+
+def exchange_kernel(
+    count,
+    peers,
+    terms_ref,
+    scale_ref,
+    grad_ref,
+    loss_ref,
+    slots,
+    loss_peer,
+    loss_ring,
+    rs_send,
+    rs_recv,
+    ag_send,
+    ag_recv,
+    lp_send,
+    lp_recv,
+    lr_send,
+    lr_recv,
+):
+    me = lax.axis_index("dp")
+    lane = lax.axis_index("mp")
+    place = ring_position(me, count)
+    right = ring_index((place + 1) % count, count)
+    left = ring_index((place + count - 1) % count, count)
+    rows, columns = slots.shape[1], slots.shape[2]
+    pieces = column_pieces(columns)
+    steps = count - 1
+
+    barrier = pltpu.get_barrier_semaphore()
+    for other in (left, right):
+        pl.semaphore_signal(barrier, inc=1, device_id={"dp": other}, device_id_type=MESH)
+    for j in range(1, peers):
+        pl.semaphore_signal(
+            barrier, inc=1, device_id={"mp": (lane + j) % peers}, device_id_type=MESH
+        )
+    pl.semaphore_wait(barrier, 2 + peers - 1)
+
+    def block_rows(position):
+        start = ring_index((position + 2 * count) % count, count) * rows
+        return pl.ds(pl.multiple_of(start, rows), rows)
+
+    def target(k):
+        return {"dp": right if k % 2 == 0 else left}
+
+    def sign(k):
+        return 1 if k % 2 == 0 else -1
+
+    def reduce_copy(k, step, source):
+        lo, hi = pieces[k]
+        return pltpu.make_async_remote_copy(
+            src_ref=source,
+            dst_ref=slots.at[step, :, lo:hi],
+            send_sem=rs_send.at[step, k],
+            recv_sem=rs_recv.at[step, k],
+            device_id=target(k),
+            device_id_type=MESH,
+        )
+
+    def gather_copy(k, step):
+        lo, hi = pieces[k]
+        part = grad_ref.at[block_rows(place - sign(k) * step), lo:hi]
+        return pltpu.make_async_remote_copy(
+            src_ref=part,
+            dst_ref=part,
+            send_sem=ag_send.at[step, k],
+            recv_sem=ag_recv.at[step, k],
+            device_id=target(k),
+            device_id_type=MESH,
+        )
+
+    def gather_arrival(k, step):
+        lo, hi = pieces[k]
+        part = grad_ref.at[block_rows(place - sign(k) * (step + 1)), lo:hi]
+        return pltpu.make_async_remote_copy(
+            src_ref=part,
+            dst_ref=part,
+            send_sem=ag_send.at[step, k],
+            recv_sem=ag_recv.at[step, k],
+            device_id=target(k),
+            device_id_type=MESH,
+        )
+
+    def loss_copy(step, slot):
+        return pltpu.make_async_remote_copy(
+            src_ref=loss_ring.at[slot],
+            dst_ref=loss_ring.at[step + 1],
+            send_sem=lr_send.at[step],
+            recv_sem=lr_recv.at[step],
+            device_id={"dp": right},
+            device_id_type=MESH,
+        )
+
+    for k, (lo, hi) in enumerate(pieces):
+        reduce_copy(k, 0, terms_ref.at[block_rows(place - sign(k)), lo:hi]).start()
+
+    def reduce_step(step, carry):
+        for k, (lo, hi) in enumerate(pieces):
+            landed = slots.at[step, :, lo:hi]
+            reduce_copy(k, step, landed).wait_recv()
+            own = terms_ref[block_rows(place - sign(k) * (step + 2)), lo:hi]
+            slots[step, :, lo:hi] = (
+                slots[step, :, lo:hi].astype(jnp.float32) + own.astype(jnp.float32)
+            ).astype(jnp.bfloat16)
+            reduce_copy(k, step + 1, landed).start()
+        return carry
+
+    lax.fori_loop(0, steps - 1, reduce_step, 0)
+
+    scale = scale_ref[...]
+    total = jnp.zeros((rows, LANES), jnp.float32)
+    for k, (lo, hi) in enumerate(pieces):
+        last = slots.at[steps - 1, :, lo:hi]
+        reduce_copy(k, steps - 1, last).wait_recv()
+        summed = slots[steps - 1, :, lo:hi].astype(jnp.float32) + terms_ref[
+            block_rows(place), lo:hi
+        ].astype(jnp.float32)
+        weighted = scale * summed
+        grad_ref[block_rows(place), lo:hi] = (2.0 * weighted).astype(jnp.bfloat16)
+        gather_copy(k, 0).start()
+        squares = weighted * summed
+        for at in range(0, hi - lo, LANES):
+            total = total + squares[:, at : at + LANES]
+
+    folded = total[:8]
+    for at in range(8, rows, 8):
+        folded = folded + total[at : at + 8]
+    loss_peer[0] = folded
+
+    def peer_copy(j):
+        return pltpu.make_async_remote_copy(
+            src_ref=loss_peer.at[0],
+            dst_ref=loss_peer.at[j],
+            send_sem=lp_send.at[j - 1],
+            recv_sem=lp_recv.at[j - 1],
+            device_id={"mp": (lane + j) % peers},
+            device_id_type=MESH,
+        )
+
+    for j in range(1, peers):
+        peer_copy(j).start()
+    for j in range(1, peers):
+        peer_copy(j).wait_recv()
+        folded = folded + loss_peer[j]
+    loss_ring[0] = folded
+    loss_copy(0, 0).start()
+
+    def gather_step(step, carry):
+        for k in range(len(pieces)):
+            gather_arrival(k, step).wait_recv()
+            gather_copy(k, step + 1).start()
+        loss_copy(step, step).wait_recv()
+        loss_copy(step + 1, step + 1).start()
+        return carry
+
+    lax.fori_loop(0, steps - 1, gather_step, 0)
+    for k in range(len(pieces)):
+        gather_arrival(k, steps - 1).wait_recv()
+    loss_copy(steps - 1, steps - 1).wait_recv()
+    loss_ref[...] = jnp.sum(loss_ring[...], axis=0)
+
+    def drain(step, carry):
+        for k, (lo, hi) in enumerate(pieces):
+            reduce_copy(k, step, slots.at[step, :, lo:hi]).wait_send()
+            gather_copy(k, step).wait_send()
+        loss_copy(step, step).wait_send()
+        return carry
+
+    lax.fori_loop(0, steps, drain, 0)
+    for j in range(1, peers):
+        peer_copy(j).wait_send()
+
+
+def exchange(terms, token_weight, count, peers):
+    rows, columns = terms.shape[0] // count, terms.shape[1]
+    steps, parts = count - 1, len(column_pieces(columns))
+    spec = pl.BlockSpec(memory_space=pltpu.VMEM)
+    dma = pltpu.SemaphoreType.DMA
+    grad, loss = pl.pallas_call(
+        functools.partial(exchange_kernel, count, peers),
+        out_shape=(
+            jax.ShapeDtypeStruct(terms.shape, jnp.bfloat16),
+            jax.ShapeDtypeStruct((8, LANES), jnp.float32),
+        ),
+        in_specs=[spec, spec],
+        out_specs=(spec, spec),
+        scratch_shapes=[
+            pltpu.VMEM((steps, rows, columns), jnp.bfloat16),
+            pltpu.VMEM((peers, 8, LANES), jnp.float32),
+            pltpu.VMEM((count, 8, LANES), jnp.float32),
+            dma((steps, parts)),
+            dma((steps, parts)),
+            dma((steps, parts)),
+            dma((steps, parts)),
+            dma((peers - 1,)),
+            dma((peers - 1,)),
+            dma((steps,)),
+            dma((steps,)),
+        ],
+        compiler_params=pltpu.CompilerParams(collective_id=0, has_side_effects=True),
+    )(terms, token_weight)
+    return grad, jnp.sum(loss)
 
 
 def soft_weight(weight, variable, channel_scale, bit_width, zero_point, fan_in):
@@ -25,6 +258,8 @@
 
 
 def shards(
+    count,
+    peers,
     tokens,
     gate_weight,
     up_weight,
@@ -62,17 +297,12 @@
     )
     down_student = soft_weight(down_weight, down_round, down_scale, down_bits, down_zero, FF)
     terms = jnp.dot(
-        hidden,
-        jnp.concatenate([-down_weight, down_student], axis=0),
-        preferred_element_type=jnp.float32,
-    )
-    summed = lax.psum_scatter(terms, "dp", scatter_dimension=0, tiled=True)
+        hidden[:, hidden_cols:], down_student, preferred_element_type=jnp.float32
+    ) - jnp.dot(hidden[:, :hidden_cols], down_weight, preferred_element_type=jnp.float32)
     token_weight = lax.dynamic_slice_in_dim(fisher, lax.axis_index("dp") * own_rows, own_rows)
-    weighted = token_weight[:, None] * summed
-    partial_loss = jnp.sum(weighted * summed)
-    local_grad = (2.0 * weighted).astype(jnp.bfloat16)
-    loss_sum = lax.psum(partial_loss, ("dp", "mp"))
-    out_grad = lax.all_gather(local_grad, "dp", axis=0, tiled=True)
+    out_grad, loss_sum = exchange(
+        terms.astype(jnp.bfloat16), token_weight[:, None], count, peers
+    )
     loss_value = loss_sum / (total_rows * D)
     grad_down = contract_rows(hidden[:, hidden_cols:], out_grad).astype(jnp.bfloat16)
     hidden_part = lax.dot_general(
@@ -87,9 +317,8 @@
     both_grads = lax.all_gather(
         jnp.concatenate([gate_grad, up_grad], axis=1), "mp", axis=0, tiled=True
     )
-    weight_grads = contract_rows(all_tokens, both_grads)
-    grad_gate = weight_grads[:, :hidden_cols].astype(jnp.bfloat16)
-    grad_up = weight_grads[:, hidden_cols:].astype(jnp.bfloat16)
+    grad_gate = contract_rows(all_tokens, both_grads[:, :hidden_cols]).astype(jnp.bfloat16)
+    grad_up = contract_rows(all_tokens, both_grads[:, hidden_cols:]).astype(jnp.bfloat16)
     return (loss_value, grad_gate, grad_up, grad_down)
 
 
@@ -111,4 +340,5 @@
         P(),
     )
     out_specs = (P(), P("mp", "dp"), P("mp", "dp"), P("dp", "mp"))
-    return jax.shard_map(shards, mesh=mesh, in_specs=in_specs, out_specs=out_specs, check_vma=False)
+    body = functools.partial(shards, mesh.shape["dp"], mesh.shape["mp"])
+    return jax.shard_map(body, mesh=mesh, in_specs=in_specs, out_specs=out_specs, check_vma=False)

time: 534 us -> 364 us (0.68)
  waiting for transfers between devices: 307 us -> 77 us
  Pallas kernels: 0 us -> 115 us
  blocking collectives: 40.9 us -> 0 us
  local copies, waits for them, and re-layouts: 35.8 us -> 24.6 us
  other arithmetic: 59.4 us -> 49.3 us
  matrix products: 73.5 us -> 80.9 us
    reduce_scatter x1 -> x0, waiting for transfers between devices: 157 us -> none  [shards(): summed = lax.psum_scatter(terms, 'dp', scatter_dimension=0, tiled=True)]
    pallas_call x0 -> x1, Pallas kernels: none -> 115 us  [exchange(): pl.pallas_call(functools.partial(exchange_kernel, count, peers), out_shap...]
    all_gather x1 -> x0, waiting for transfers between devices: 74.7 us -> none  [shards(): out_grad = lax.all_gather(local_grad, 'dp', axis=0, tiled=True)]
    psum x1 -> x0, blocking collectives: 40.9 us -> none  [shards(): loss_sum = lax.psum(partial_loss, ('dp', 'mp'))]
    slice x1 -> x0, local copies, waits for them, and re-layouts: 11.4 us -> none  [shards(): grad_up = weight_grads[:, hidden_cols:].astype(jnp.bfloat16)]
    neg x1 -> x0, other arithmetic: 8.2 us -> none  [shards(): -down_weight]
    dot_general x2 -> x3, matrix products: 23.1 us -> 27.6 us  [contract_rows(): lax.dot_general(left, right, (((0,), (0,)), ((), ())), preferred_element_...]
    dot_general x1 -> x2, matrix products: 15 us -> 18 us  [the longest x1 10 us: shards(): jnp.dot(hidden[:, :hidden_cols], down_weight, preferred_element_type=jnp....]
  transfers between devices with their start and end apart: 7 -> 5, of which waited for: 5 -> 4; matrix products, arithmetic and copies ran while one was open for 11% -> 14% of each run, Pallas kernels for 0% -> 0%
where the time goes in v1:
time: 364 us; the launch traced here: 363 us
  Pallas kernels  115 us (32%)
  matrix products  80.9 us (22%)
  waiting for transfers between devices  77 us (21%)
  other arithmetic  49.3 us (14%)
  local copies, waits for them, and re-layouts  24.6 us (7%)
  between operations  15.6 us (4%)
    pallas_call x1, Pallas kernels, exchange(): pl.pallas_call(functools.partial(exchange_kernel, count, peers), out_shap...  115 us
    all_gather x1, waiting for transfers between devices, shards(): all_tokens = lax.all_gather(tokens, 'dp', axis=0, tiled=True)  50.4 us
    convert_element_type x2, other arithmetic, soft_weight(): return (quant_step * (levels - zero_level)).astype(jnp.bfloat16)  38.6 us
    dot_general x3, matrix products, contract_rows(): lax.dot_general(left, right, (((0,), (0,)), ((), ())), preferred_element_...  27.6 us
    dot_general x1, matrix products, shards(): jnp.dot(all_tokens, stacked, preferred_element_type=jnp.float32)  25 us
    unnamed x18, local copies, waits for them, and re-layouts  23.8 us
    reduce_scatter x1, waiting for transfers between devices, shards(): lax.psum_scatter(partial_value, 'mp', scatter_dimension=0, tiled=True)  15 us
    dot_general x1, matrix products, shards(): lax.dot_general(out_grad, down_student, (((1,), (1,)), ((), ())), preferr...  10.3 us
  transfers between devices with their start and end apart: 5, of which 4 were waited for; matrix products, arithmetic and copies ran while one was open for 14% of the time, Pallas kernels for 0%

profile of v1, /device:TPU:0, one launch (start us, length us, event | category | flops | bytes accessed | tf_op | source)
XLA Modules:
  0.0 363.3 jit_solution(11233273766346269850)
XLA Ops:
  7.2 0.0 copy-start
  7.2 0.0 all-gather.4.cloned.1.call-start
  7.2 0.7 all-gather.4.cloned.1.call-update
  7.9 0.0 reduce-scatter.3.cloned.1.call-start
  8.0 0.8 multiply_reduce_fusion.1
  8.8 0.8 convert_reduce_fusion.3
  9.6 0.8 convert_reduce_fusion.2
  10.4 24.4 %multiply_convert_fusion.1 = (bf16[3584,1152]{1,0:T(8,128)(2,1)}, bf16[3584,1152]{1,0:T(8,128)(2,1)}) fusion(bf16[3584,1152]{1,0:T(8,128)(2,1)} %param.19, bf16[3584,1152]{1,0:T(8,128)(2,1)} %param.16, f32[1152]{0:T(1024)S(1)} %get-tuple-element.17, f32[1152]{0:T(1024)S(1)} %get-tuple-element.15, f32[1152]{0:T(1024)S(1)} %get-tuple-element.13, ...), kind=kLoop, calls=%fused_computation.9 | loop fusion | flops 140378112 | bytes 49572864 | tf_op jit(solution)/shard_map/convert_element_type | solution.py:251
  34.8 50.4 %all-gather.4.cloned.1.call-done = bf16[512,3584]{1,0:T(8,128)(2,1)} async-done(((bf16[32,3584]{1,0:T(8,128)(2,1)}), bf16[512,3584]{1,0:T(8,128)(2,1)}) %all-gather.4.cloned.1.call-update) | async-done | bytes 3670032 | tf_op jit(solution)/shard_map/all_gather | solution.py:280
  85.1 25.0 %fusion.10 = f32[512,4608]{0,1:T(8,128)} fusion(bf16[512,3584]{1,0:T(8,128)(2,1)} %all-gather.4.cloned.1.call-done, bf16[3584,1152]{1,0:T(8,128)(2,1)} %get-tuple-element.22, bf16[3584,1152]{1,0:T(8,128)(2,1)} %get-tuple-element.23, bf16[3584,1152]{1,0:T(8,128)(2,1)} %param.16, bf16[3584,1152]{1,0:T(8,128)(2,1)} %param.15), kind=kOutput, calls=%fused_computation.16 | convolution fusion | flops 17043554304 | bytes 46137344 | tf_op jit(solution)/shard_map/dot_general | solution.py:287
  110.1 0.0 copy-start.3
  110.2 0.0 copy-start.4
  110.2 0.0 copy-start.5
  110.2 0.0 reduce-scatter.3.cloned.1.call-update
  110.2 0.0 all-gather.6.cloned.1.call-start
  110.2 0.6 copy-done.3
  110.9 0.0 copy-done.4
  110.9 0.0 copy-done.5
  110.9 15.0 %reduce-scatter.3.cloned.1.call-done = f32[256,4608]{0,1:T(8,128)} async-done(((f32[512,4608]{0,1:T(8,128)}), f32[256,4608]{0,1:T(8,128)}) %reduce-scatter.3.cloned.1.call-update) | async-done | bytes 4718608 | tf_op jit(solution)/shard_map/reduce_scatter | solution.py:288
  125.9 3.0 fusion.16
  129.0 1.1 pad_maximum_fusion
  130.0 0.0 all-gather.6.cloned.1.call-update
  130.1 0.2 reduce-scatter.5.cloned.1.call-start
  130.3 14.2 %multiply_convert_fusion = bf16[1152,3584]{1,0:T(8,128)(2,1)} fusion(bf16[1152,3584]{1,0:T(8,128)(2,1)} %param.20, bf16[1152,3584]{1,0:T(8,128)(2,1)} %param.17, f32[3584]{0:T(1024)S(1)} %convert_element_type.94, f32[3584]{0:T(1024)S(1)} %add_convert_fusion, f32[3584]{0:T(1024)S(1)} %broadcast_multiply_fusion), kind=kLoop, calls=%fused_computation.8 | loop fusion | flops 70189056 | bytes 24815616 | tf_op jit(solution)/shard_map/convert_element_type | solution.py:251
  144.5 0.0 copy-done
  144.5 0.1 dynamic-slice_bitcast_fusion
  144.6 0.7 copy.18.scale_ref
  145.3 7.9 %fusion.18 = f32[512,3584]{1,0:T(8,128)S(1)} fusion(bf16[1152,3584]{1,0:T(8,128)(2,1)} %multiply_convert_fusion, bf16[512,2304]{0,1:T(8,128)(2,1)} %all-gather.6.cloned.1.call-done), kind=kOutput, calls=%fused_computation.30 | convolution fusion | flops 4227858432 | bytes 16777216 | tf_op jit(solution)/shard_map/dot_general | solution.py:299
  153.2 0.0 copy-done.2
  153.3 10.0 %subtract_convert_fusion.terms_ref = bf16[512,3584]{1,0:T(8,128)(2,1)} fusion(f32[512,3584]{1,0:T(8,128)S(1)} %fusion.18, bf16[1152,3584]{1,0:T(8,128)(2,1)} %param.17, bf16[512,2304]{0,1:T(8,128)(2,1)S(1)} %copy-done.2), kind=kOutput, calls=%fused_computation.17 | convolution fusion | flops 4231528448 | bytes 20447232 | tf_op jit(solution)/shard_map/dot_general | solution.py:301
  163.3 115.2 %shard_map.165 = (bf16[512,3584]{1,0:T(8,128)(2,1)}, f32[8,128]{1,0:T(8,128)}) custom-call(bf16[512,3584]{1,0:T(8,128)(2,1)} %subtract_convert_fusion.terms_ref, f32[32,1]{1,0:T(8,128)} %copy.18.scale_ref), custom_call_target="tpu_custom_call" | custom-call | tf_op jit(solution)/shard_map/pallas_call | solution.py:217
  278.5 10.3 %fusion.21 = f32[512,1152]{0,1:T(8,128)} fusion(bf16[512,3584]{1,0:T(8,128)(2,1)} %get-tuple-element.7, bf16[1152,3584]{1,0:T(8,128)(2,1)} %multiply_convert_fusion), kind=kOutput, calls=%fused_computation.42 | convolution fusion | flops 4227858432 | bytes 14286848 | tf_op jit(solution)/shard_map/dot_general | solution.py:308
  288.8 0.0 reduce-scatter.5.cloned.1.call-update
  288.8 0.3 all-gather.8.cloned.1.call-start
  289.1 8.9 %reduce-scatter.5.cloned.1.call-done = f32[256,1152]{0,1:T(8,128)} async-done(((f32[512,1152]{0,1:T(8,128)}), f32[256,1152]{0,1:T(8,128)}) %reduce-scatter.5.cloned.1.call-update) | async-done | bytes 1179664 | tf_op jit(solution)/shard_map/reduce_scatter | solution.py:311
  298.0 2.5 multiply_convert_fusion.4
  300.6 1.1 pad_maximum_fusion.1
  301.7 0.0 all-gather.8.cloned.1.call-update
  301.7 0.0 copy-done.6
  301.7 0.6 reduce_sum.9
  302.9 8.7 %convolution_convert_fusion = bf16[1152,3584]{1,0:T(8,128)(2,1)} fusion(bf16[512,3584]{1,0:T(8,128)(2,1)} %get-tuple-element.7, bf16[512,2304]{0,1:T(8,128)(2,1)S(1)} %copy-done.2), kind=kOutput, calls=%fused_computation.11 | convolution fusion | flops 4231987200 | bytes 13107200 | tf_op jit(solution)/shard_map/dot_general | solution.py:255
  311.7 1.9 all-gather.8.cloned.1.call-done
  313.6 10.2 %fusion.9 = bf16[3584,1152]{0,1:T(8,128)(2,1)} fusion(bf16[512,3584]{1,0:T(8,128)(2,1)} %all-gather.4.cloned.1.call-done, bf16[512,2304]{0,1:T(8,128)(2,1)} %all-gather.8.cloned.1.call-done), kind=kOutput, calls=%fused_computation.15 | convolution fusion | flops 4231987200 | bytes 13107200 | tf_op jit(solution)/shard_map/dot_general | solution.py:255
  323.8 11.7 %copy.21 = bf16[3584,1152]{1,0:T(8,128)(2,1)} copy(bf16[3584,1152]{0,1:T(8,128)(2,1)} %fusion.9) | data formatting | bytes 16515072
  335.4 0.0 copy-done.7
  335.4 8.7 %fusion.8 = bf16[3584,1152]{0,1:T(8,128)(2,1)} fusion(bf16[512,3584]{1,0:T(8,128)(2,1)} %all-gather.4.cloned.1.call-done, bf16[512,2304]{0,1:T(8,128)(2,1)S(1)} %copy-done.7), kind=kOutput, calls=%fused_computation.14 | convolution fusion | flops 4231987200 | bytes 13107200 | tf_op jit(solution)/shard_map/dot_general | solution.py:255
  344.1 11.5 %copy.20 = bf16[3584,1152]{1,0:T(8,128)(2,1)} copy(bf16[3584,1152]{0,1:T(8,128)(2,1)} %fusion.8) | data formatting | bytes 16515072
  355.6 0.0 copy-done.1
  (8 shorter events, 0.0 us)
Async XLA Ops:
  7.2 137.4 %copy-start = (f32[512]{0:T(512)S(1)}, f32[512]{0:T(512)}, u32[]{:S(2)}) copy-start(f32[512]{0:T(512)} %param.27) | copy-start | bytes 6148
  7.2 77.9 %all-gather.4.cloned.1.call-start = ((), (), s32[]{:S(2)}) async-start(), calls=%async_computation.2 | async-start | bytes 3899392 | tf_op jit(solution)/shard_map/all_gather | solution.py:280
  7.9 118.0 %reduce-scatter.3.cloned.1.call-start = ((), (), s32[]{:S(2)}) async-start(), calls=%async_computation.3 | async-start | bytes 14155776 | tf_op jit(solution)/shard_map/reduce_scatter | solution.py:288
  110.1 0.7 copy-start.3
  110.2 0.7 copy-start.4
  110.2 0.7 copy-start.5
  110.2 35.1 %all-gather.6.cloned.1.call-start = ((), (), s32[]{:S(2)}) async-start(), calls=%async_computation.4 | async-start | bytes 3538944 | tf_op jit(solution)/shard_map/all_gather | solution.py:295
  130.1 168.0 %reduce-scatter.5.cloned.1.call-start = ((), (), s32[]{:S(2)}) async-start(), calls=%async_computation.5 | async-start | bytes 3538944 | tf_op jit(solution)/shard_map/reduce_scatter | solution.py:311
  145.3 7.9 %copy-start.2 = (bf16[512,2304]{0,1:T(8,128)(2,1)S(1)}, bf16[512,2304]{0,1:T(8,128)(2,1)}, u32[]{:S(2)}) copy-start(bf16[512,2304]{0,1:T(8,128)(2,1)} %all-gather.6.cloned.1.call-done) | copy-start | bytes 7077892
  288.8 12.9 %copy-start.6 = (f32[8,128]{1,0:T(8,128)S(1)}, f32[8,128]{1,0:T(8,128)}, u32[]{:S(2)}) copy-start(f32[8,128]{1,0:T(8,128)} %get-tuple-element.6) | copy-start | bytes 12292
  288.8 24.7 %all-gather.8.cloned.1.call-start = ((), (), s32[]{:S(2)}) async-start(), calls=%async_computation.6 | async-start | bytes 3538944 | tf_op jit(solution)/shard_map/all_gather | solution.py:317
  323.8 11.7 %copy-start.7 = (bf16[512,2304]{0,1:T(8,128)(2,1)S(1)}, bf16[512,2304]{0,1:T(8,128)(2,1)}, u32[]{:S(2)}) copy-start(bf16[512,2304]{0,1:T(8,128)(2,1)} %all-gather.8.cloned.1.call-done) | copy-start | bytes 7077892
  335.4 20.2 %copy-start.1 = (f32[512]{0:T(512)S(1)}, f32[512]{0:T(512)}, u32[]{:S(2)}) copy-start(f32[512]{0:T(512)} %param.27) | copy-start | bytes 6148
Sparse Core Ops, SparseCore 0:
  10.7 74.3 all-gather.3
  110.3 15.5 reduce-scatter.2
  130.2 11.7 all-gather.5
  289.0 9.0 reduce-scatter.4
  301.8 11.7 all-gather.7

commit v2 on v1

--- a/solution.py
+++ b/solution.py
@@ -4,6 +4,7 @@
 import jax.numpy as jnp
 from jax import lax
 from jax.experimental import pallas as pl
+from jax.experimental.layout import Layout, with_layout_constraint
 from jax.experimental.pallas import tpu as pltpu
 from jax.sharding import PartitionSpec as P
 
@@ -31,7 +32,7 @@
     return column * depth + level + (column % 2) * (depth - 1 - 2 * level)
 
 
-def column_pieces(columns, parts=4):
+def column_pieces(columns, parts=8):
     tiles = columns // LANES
     edges = [tiles * k // parts * LANES for k in range(parts)] + [columns]
     return [(lo, hi) for lo, hi in zip(edges[:-1], edges[1:]) if hi > lo]
@@ -78,11 +79,14 @@
         start = ring_index((position + 2 * count) % count, count) * rows
         return pl.ds(pl.multiple_of(start, rows), rows)
 
+    turn = 1 - 2 * (lane % 2)
+    onward = ring_index((place + turn + count) % count, count)
+
     def target(k):
-        return {"dp": right if k % 2 == 0 else left}
+        return {"dp": onward}
 
     def sign(k):
-        return 1 if k % 2 == 0 else -1
+        return turn
 
     def reduce_copy(k, step, source):
         lo, hi = pieces[k]
@@ -125,7 +129,7 @@
             dst_ref=loss_ring.at[step + 1],
             send_sem=lr_send.at[step],
             recv_sem=lr_recv.at[step],
-            device_id={"dp": right},
+            device_id={"dp": onward},
             device_id_type=MESH,
         )
 
@@ -238,6 +242,146 @@
         compiler_params=pltpu.CompilerParams(collective_id=0, has_side_effects=True),
     )(terms, token_weight)
     return grad, jnp.sum(loss)
+
+
+def gather_kernel(
+    count,
+    stride,
+    tokens_ref,
+    channel_ref,
+    gate_ref,
+    gate_round_ref,
+    up_ref,
+    up_round_ref,
+    gate_out,
+    up_out,
+    all_ref,
+    held,
+    send_sem,
+    recv_sem,
+    local_sem,
+):
+    at = pl.program_id(0)
+    last = pl.num_programs(0) - 1
+    me = lax.axis_index("dp")
+    place = ring_position(me, count)
+    right = ring_index((place + 1) % count, count)
+    left = ring_index((place + count - 1) % count, count)
+    rows, columns = tokens_ref.shape
+    pieces = column_pieces(columns)
+    steps = count - 1
+    sign = 1 - 2 * (lax.axis_index("mp") % 2)
+    onward = ring_index((place + sign + count) % count, count)
+
+    def ring_copy(k, step, hop):
+        lo, hi = pieces[k]
+        start = ring_index((place - sign * (step + hop) + 2 * count) % count, count) * rows
+        part = held.at[pl.ds(pl.multiple_of(start, rows), rows), lo:hi]
+        return pltpu.make_async_remote_copy(
+            src_ref=part,
+            dst_ref=part,
+            send_sem=send_sem.at[step, k],
+            recv_sem=recv_sem.at[step, k],
+            device_id={"dp": onward},
+            device_id_type=MESH,
+        )
+
+    @pl.when(at == 0)
+    def _():
+        own = pltpu.make_async_copy(
+            tokens_ref, held.at[pl.ds(pl.multiple_of(me * rows, rows), rows), :], local_sem
+        )
+        own.start()
+        barrier = pltpu.get_barrier_semaphore()
+        for other in (left, right):
+            pl.semaphore_signal(barrier, inc=1, device_id={"dp": other}, device_id_type=MESH)
+        pl.semaphore_wait(barrier, 2)
+        own.wait()
+        for k in range(len(pieces)):
+            ring_copy(k, 0, 0).start()
+
+    def relay(step, carry):
+        for k in range(len(pieces)):
+            ring_copy(k, step, 1).wait_recv()
+            ring_copy(k, step + 1, 0).start()
+        return carry
+
+    @pl.when((at > 0) & (at % stride == 0) & (at // stride < steps))
+    def _():
+        relay(at // stride - 1, 0)
+
+    chunk = 16
+    tile = gate_ref.shape[0]
+
+    def weights(step, carry):
+        here = pl.ds(pl.multiple_of(step * chunk, chunk), chunk)
+        for row, weight, rounding, out in (
+            (0, gate_ref, gate_round_ref, gate_out),
+            (1, up_ref, up_round_ref, up_out),
+        ):
+            unit, inverse, low, high = (channel_ref[4 * row + j : 4 * row + j + 1] for j in range(4))
+            spread = jnp.tanh(0.5 * rounding[here, :].astype(jnp.float32))
+            offset = jnp.clip(0.6 * spread, -0.5, 0.5)
+            levels = weight[here, :].astype(jnp.float32) * inverse + offset
+            levels = jnp.minimum(jnp.maximum(levels, low), high)
+            out[here, :] = (unit * levels).astype(jnp.bfloat16)
+        return carry
+
+    lax.fori_loop(0, tile // chunk, weights, 0)
+
+    @pl.when(at == last)
+    def _():
+        reached = jnp.minimum(last // stride, steps - 1)
+        lax.fori_loop(reached, steps - 1, relay, 0)
+        for k in range(len(pieces)):
+            ring_copy(k, steps - 1, 1).wait_recv()
+        done = pltpu.make_async_copy(held, all_ref, local_sem)
+        done.start()
+
+        def drain(step, carry):
+            for k in range(len(pieces)):
+                ring_copy(k, step, 0).wait_send()
+            return carry
+
+        lax.fori_loop(0, steps, drain, 0)
+        done.wait()
+
+
+def gather_and_round(tokens, weights, rounds, scale, bits, zero, count):
+    rows, columns = tokens.shape
+    depth, width = weights[0].shape
+    steps, parts = count - 1, len(column_pieces(columns))
+    tiles = max(g for g in range(1, 33) if depth % (16 * g) == 0)
+    tile = depth // tiles
+    root = jnp.sqrt(jnp.float32(D))
+    unit = scale / root
+    zero_level = zero.astype(jnp.float32)
+    ceiling = (jnp.left_shift(jnp.int32(1), bits) - 1).astype(jnp.float32)
+    channel = jnp.stack([unit, 1.0 / unit, -zero_level, ceiling - zero_level], axis=1)
+    channel = channel.reshape(8, width)
+    block = pl.BlockSpec((tile, width), lambda i: (i, 0))
+    anywhere = pl.BlockSpec(memory_space=pl.ANY)
+    dma = pltpu.SemaphoreType.DMA
+    return pl.pallas_call(
+        functools.partial(gather_kernel, count, max(1, tiles // count)),
+        grid=(tiles,),
+        out_shape=(
+            jax.ShapeDtypeStruct((depth, width), jnp.bfloat16),
+            jax.ShapeDtypeStruct((depth, width), jnp.bfloat16),
+            jax.ShapeDtypeStruct((count * rows, columns), jnp.bfloat16),
+        ),
+        in_specs=[anywhere, pl.BlockSpec((8, width), lambda i: (0, 0))] + [block] * 4,
+        out_specs=(block, block, anywhere),
+        scratch_shapes=[
+            pltpu.VMEM((count * rows, columns), jnp.bfloat16),
+            dma((steps, parts)),
+            dma((steps, parts)),
+            dma(()),
+        ],
+        compiler_params=pltpu.CompilerParams(
+            collective_id=1, has_side_effects=True, dimension_semantics=("arbitrary",)
+        ),
+    )(tokens, channel, weights[0], rounds[0], weights[1], rounds[1])
 
 
 def soft_weight(weight, variable, channel_scale, bit_width, zero_point, fan_in):
@@ -277,12 +421,17 @@
 ):
     own_rows = tokens.shape[0]
     hidden_cols = gate_weight.shape[1]
-    all_tokens = lax.all_gather(tokens, "dp", axis=0, tiled=True)
+    gate_student, up_student, all_tokens = gather_and_round(
+        tokens,
+        (gate_weight, up_weight),
+        (gate_round, up_round),
+        quant_scale,
+        quant_bits,
+        quant_zero,
+        count,
+    )
     total_rows = all_tokens.shape[0]
-    gate_student = soft_weight(
-        gate_weight, gate_round, quant_scale[0], quant_bits[0], quant_zero[0], D
-    )
-    up_student = soft_weight(up_weight, up_round, quant_scale[1], quant_bits[1], quant_zero[1], D)
+
     stacked = jnp.concatenate([gate_weight, up_weight, gate_student, up_student], axis=1)
     partial_value = jnp.dot(all_tokens, stacked, preferred_element_type=jnp.float32)
     shares = lax.psum_scatter(partial_value, "mp", scatter_dimension=0, tiled=True)
@@ -308,7 +457,9 @@
     hidden_part = lax.dot_general(
         out_grad, down_student, (((1,), (1,)), ((), ())), preferred_element_type=jnp.float32
     )
-    hidden_grad = lax.psum_scatter(hidden_part, "mp", scatter_dimension=0, tiled=True)
+    hidden_grad = lax.psum_scatter(
+        hidden_part.astype(jnp.bfloat16), "mp", scatter_dimension=0, tiled=True
+    ).astype(jnp.float32)
     sigmoid_gate = jax.nn.sigmoid(gate_own)
     gate_grad = (
         hidden_grad * up_own * sigmoid_gate * (1.0 + gate_own * (1.0 - sigmoid_gate))
@@ -319,6 +470,8 @@
     )
     grad_gate = contract_rows(all_tokens, both_grads[:, :hidden_cols]).astype(jnp.bfloat16)
     grad_up = contract_rows(all_tokens, both_grads[:, hidden_cols:]).astype(jnp.bfloat16)
+    grad_gate = with_layout_constraint(grad_gate, Layout((0, 1)))
+    grad_up = with_layout_constraint(grad_up, Layout((0, 1)))
     return (loss_value, grad_gate, grad_up, grad_down)
 
 

time: 364 us -> 313 us (0.86)
  Pallas kernels: 115 us -> 166 us
  waiting for transfers between devices: 77 us -> 26 us
  other arithmetic: 49.3 us -> 23.1 us
  local copies, waits for them, and re-layouts: 24.6 us -> 2.1 us
    pallas_call x0 -> x1, Pallas kernels: none -> 64.7 us  [gather_and_round(): pl.pallas_call(functools.partial(gather_kernel, count, max(1, tiles // co...]
    all_gather x1 -> x0, waiting for transfers between devices: 50.4 us -> none  [shards(): all_tokens = lax.all_gather(tokens, 'dp', axis=0, tiled=True)]
    convert_element_type x2 -> x1, other arithmetic: 38.6 us -> 14.1 us  [soft_weight(): return (quant_step * (levels - zero_level)).astype(jnp.bfloat16)]
    unnamed x18, local copies, waits for them, and re-layouts: 23.8 us -> 0.69 us
    pallas_call x1, Pallas kernels: 115 us -> 101 us  [exchange(): pl.pallas_call(functools.partial(exchange_kernel, count, peers), out_shap...]
  transfers between devices with their start and end apart: 5 -> 4, of which waited for: 4 -> 3; matrix products, arithmetic and copies ran while one was open for 14% -> 8% of each run, Pallas kernels for 0% -> 0%
where the time goes in v2:
time: 313 us; the launch traced here: 312 us
  Pallas kernels  166 us (53%)
  matrix products  79.3 us (25%)
  waiting for transfers between devices  26 us (8%)
  other arithmetic  23.1 us (7%)
  between operations  15.7 us (5%)
    pallas_call x1, Pallas kernels, exchange(): pl.pallas_call(functools.partial(exchange_kernel, count, peers), out_shap...  101 us
    pallas_call x1, Pallas kernels, gather_and_round(): pl.pallas_call(functools.partial(gather_kernel, count, max(1, tiles // co...  64.7 us
    dot_general x3, matrix products, contract_rows(): lax.dot_general(left, right, (((0,), (0,)), ((), ())), preferred_element_...  26.6 us
    dot_general x1, matrix products, shards(): jnp.dot(all_tokens, stacked, preferred_element_type=jnp.float32)  24.7 us
    reduce_scatter x1, waiting for transfers between devices, shards(): lax.psum_scatter(partial_value, 'mp', scatter_dimension=0, tiled=True)  15.9 us
    convert_element_type x1, other arithmetic, soft_weight(): return (quant_step * (levels - zero_level)).astype(jnp.bfloat16)  14.1 us
    dot_general x1, matrix products, shards(): lax.dot_general(out_grad, down_student, (((1,), (1,)), ((), ())), preferr...  10.4 us
    dot_general x1, matrix products, shards(): jnp.dot(hidden[:, :hidden_cols], down_weight, preferred_element_type=jnp....  9.84 us
  transfers between devices with their start and end apart: 4, of which 3 were waited for; matrix products, arithmetic and copies ran while one was open for 8% of the time, Pallas kernels for 0%

profile of v2, /device:TPU:0, one launch (start us, length us, event | category | flops | bytes accessed | tf_op | source)
XLA Modules:
  0.0 312.4 jit_solution(11269112493081104871)
XLA Ops:
  7.2 0.0 copy-start
  7.2 0.0 reduce-scatter.3.cloned.1.call-start
  7.2 0.8 negate_bitcast_fusion
  8.0 0.6 reshape.14.channel_ref
  8.7 64.7 %shard_map.165 = (bf16[3584,1152]{1,0:T(8,128)(2,1)}, bf16[3584,1152]{1,0:T(8,128)(2,1)}, bf16[512,3584]{1,0:T(8,128)(2,1)}) custom-call(bf16[32,3584]{1,0:T(8,128)(2,1)} %tokens_ref.1, f32[8,1152]{1,0:T(8,128)} %reshape.14.channel_ref, bf16[3584,1152]{1,0:T(8,128)(2,1)} %gate_ref.1, bf16[3584,1152]{1,0:T(8,128)(2,1)} %gate_round_ref.1, ...), custom_call_target="tpu_custom_call" | custom-call | tf_op jit(solution)/shard_map/pallas_call | solution.py:365
  73.3 24.7 %fusion = f32[512,4608]{1,0:T(8,128)} fusion(bf16[512,3584]{1,0:T(8,128)(2,1)} %get-tuple-element.9, bf16[3584,1152]{1,0:T(8,128)(2,1)} %get-tuple-element.11, bf16[3584,1152]{1,0:T(8,128)(2,1)} %get-tuple-element.10, bf16[3584,1152]{1,0:T(8,128)(2,1)} %up_ref.1, bf16[3584,1152]{1,0:T(8,128)(2,1)} %gate_ref.1), kind=kOutput, calls=%fused_computation | convolution fusion | flops 17043554304 | bytes 46137344 | tf_op jit(solution)/shard_map/dot_general | solution.py:436
  98.0 0.0 copy-start.2
  98.0 0.0 copy-start.3
  98.0 0.0 copy-start.4
  98.0 0.0 reduce-scatter.3.cloned.1.call-update
  98.0 0.0 all-gather.3.cloned.1.call-start
  98.1 0.6 copy-done.2
  98.7 0.0 copy-done.3
  98.8 0.0 copy-done.4
  98.8 15.9 %reduce-scatter.3.cloned.1.call-done = f32[256,4608]{1,0:T(8,128)} async-done(((f32[512,4608]{1,0:T(8,128)}), f32[256,4608]{1,0:T(8,128)}) %reduce-scatter.3.cloned.1.call-update) | async-done | bytes 4718608 | tf_op jit(solution)/shard_map/reduce_scatter | solution.py:437
  114.7 3.0 fusion.16
  117.7 1.1 pad_maximum_fusion
  118.8 0.0 all-gather.3.cloned.1.call-update
  118.8 0.2 reduce-scatter.5.cloned.1.call-start
  119.0 14.1 %multiply_convert_fusion = bf16[1152,3584]{1,0:T(8,128)(2,1)} fusion(bf16[1152,3584]{1,0:T(8,128)(2,1)} %param.20, bf16[1152,3584]{1,0:T(8,128)(2,1)} %param.17, f32[3584]{0:T(1024)S(1)} %convert_element_type.58, f32[3584]{0:T(1024)S(1)} %add_convert_fusion, f32[3584]{0:T(1024)S(1)} %broadcast_multiply_fusion), kind=kLoop, calls=%fused_computation.8 | loop fusion | flops 70189056 | bytes 24815616 | tf_op jit(solution)/shard_map/convert_element_type | solution.py:395
  133.2 0.0 copy-done
  133.2 0.1 dynamic-slice_bitcast_fusion
  133.3 0.7 copy.19.scale_ref
  133.9 0.0 all-gather.3.cloned.1.call-done
  134.0 0.0 copy-start.7
  134.0 7.8 %fusion.18 = f32[512,3584]{1,0:T(8,128)S(1)} fusion(bf16[1152,3584]{1,0:T(8,128)(2,1)} %multiply_convert_fusion, bf16[512,2304]{1,0:T(8,128)(2,1)} %all-gather.3.cloned.1.call-done), kind=kOutput, calls=%fused_computation.31 | convolution fusion | flops 4227858432 | bytes 16777216 | tf_op jit(solution)/shard_map/dot_general | solution.py:448
  141.7 0.0 copy-done.7
  141.8 9.8 %subtract_convert_fusion.terms_ref = bf16[512,3584]{1,0:T(8,128)(2,1)} fusion(f32[512,3584]{1,0:T(8,128)S(1)} %fusion.18, bf16[1152,3584]{1,0:T(8,128)(2,1)} %param.17, bf16[512,2304]{1,0:T(8,128)(2,1)S(1)} %copy-done.7), kind=kOutput, calls=%fused_computation.12 | convolution fusion | flops 4231528448 | bytes 20447232 | tf_op jit(solution)/shard_map/dot_general | solution.py:450
  151.6 101.1 %shard_map.166 = (bf16[512,3584]{1,0:T(8,128)(2,1)}, f32[8,128]{1,0:T(8,128)}) custom-call(bf16[512,3584]{1,0:T(8,128)(2,1)} %subtract_convert_fusion.terms_ref, f32[32,1]{1,0:T(8,128)} %copy.19.scale_ref), custom_call_target="tpu_custom_call" | custom-call | tf_op jit(solution)/shard_map/pallas_call | solution.py:221
  252.7 10.4 %convolution_convert_fusion.3 = bf16[512,1152]{1,0:T(8,128)(2,1)} fusion(bf16[512,3584]{1,0:T(8,128)(2,1)} %get-tuple-element.13, bf16[1152,3584]{1,0:T(8,128)(2,1)} %multiply_convert_fusion), kind=kOutput, calls=%fused_computation.13 | convolution fusion | flops 4228448256 | bytes 13107200 | tf_op jit(solution)/shard_map/dot_general | solution.py:457
  263.1 0.0 reduce-scatter.5.cloned.1.call-update
  263.1 0.0 copy-start.5
  263.1 0.3 all-gather.5.cloned.1.call-start
  263.4 7.4 %reduce-scatter.5.cloned.1.call-done = bf16[256,1152]{1,0:T(8,128)(2,1)} async-done(((bf16[512,1152]{1,0:T(8,128)(2,1)}), bf16[256,1152]{1,0:T(8,128)(2,1)}) %reduce-scatter.5.cloned.1.call-update) | async-done | bytes 589840 | tf_op jit(solution)/shard_map/reduce_scatter | solution.py:460
  270.8 2.4 fusion.10
  273.1 1.1 pad_maximum_fusion.1
  274.2 0.0 all-gather.5.cloned.1.call-update
  274.2 0.0 copy-done.5
  274.2 0.6 reduce_sum.9
  275.5 8.5 %convolution_convert_fusion = bf16[1152,3584]{1,0:T(8,128)(2,1)} fusion(bf16[512,3584]{1,0:T(8,128)(2,1)} %get-tuple-element.13, bf16[512,2304]{1,0:T(8,128)(2,1)S(1)} %copy-done.7), kind=kOutput, calls=%fused_computation.9 | convolution fusion | flops 4231987200 | bytes 13107200 | tf_op jit(solution)/shard_map/dot_general | solution.py:399
  284.0 2.6 all-gather.5.cloned.1.call-done
  286.6 0.0 copy-start.6
  286.6 0.0 copy-start.8
  286.6 10.8 %convolution_convert_fusion.1 = bf16[3584,1152]{1,0:T(8,128)(2,1)} fusion(bf16[512,3584]{1,0:T(8,128)(2,1)} %get-tuple-element.9, bf16[512,2304]{1,0:T(8,128)(2,1)} %all-gather.5.cloned.1.call-done), kind=kOutput, calls=%fused_computation.10 | convolution fusion | flops 4231987200 | bytes 13107200 | tf_op jit(solution)/shard_map/dot_general | solution.py:399
  297.5 0.0 copy-done.6
  297.5 0.0 copy-done.8
  297.5 7.2 %convolution_convert_fusion.2 = bf16[3584,1152]{1,0:T(8,128)(2,1)} fusion(bf16[512,3584]{1,0:T(8,128)(2,1)S(1)} %copy-done.6, bf16[512,2304]{1,0:T(8,128)(2,1)S(1)} %copy-done.8), kind=kOutput, calls=%fused_computation.11 | convolution fusion | flops 4231987200 | bytes 13107200 | tf_op jit(solution)/shard_map/dot_general | solution.py:399
  304.7 0.0 copy-done.1
  (6 shorter events, 0.0 us)
Async XLA Ops:
  7.2 126.0 %copy-start = (f32[512]{0:T(512)S(1)}, f32[512]{0:T(512)}, u32[]{:S(2)}) copy-start(f32[512]{0:T(512)} %param.27) | copy-start | bytes 6148
  7.2 107.5 %reduce-scatter.3.cloned.1.call-start = ((), (), s32[]{:S(2)}) async-start(), calls=%async_computation.2 | async-start | bytes 14155776 | tf_op jit(solution)/shard_map/reduce_scatter | solution.py:437
  98.0 0.7 copy-start.2
  98.0 0.7 copy-start.3
  98.0 0.7 copy-start.4
  98.0 35.9 %all-gather.3.cloned.1.call-start = ((), (), s32[]{:S(2)}) async-start(), calls=%async_computation.3 | async-start | bytes 3538944 | tf_op jit(solution)/shard_map/all_gather | solution.py:444
  118.8 151.9 %reduce-scatter.5.cloned.1.call-start = ((), (), s32[]{:S(2)}) async-start(), calls=%async_computation.4 | async-start | bytes 1769472 | tf_op jit(solution)/shard_map/reduce_scatter | solution.py:460
  134.0 7.8 %copy-start.7 = (bf16[512,2304]{1,0:T(8,128)(2,1)S(1)}, bf16[512,2304]{1,0:T(8,128)(2,1)}, u32[]{:S(2)}) copy-start(bf16[512,2304]{1,0:T(8,128)(2,1)} %all-gather.3.cloned.1.call-done) | copy-start | bytes 7077892
  263.1 11.1 %copy-start.5 = (f32[8,128]{1,0:T(8,128)S(1)}, f32[8,128]{1,0:T(8,128)}, u32[]{:S(2)}) copy-start(f32[8,128]{1,0:T(8,128)} %get-tuple-element.12) | copy-start | bytes 12292
  263.1 23.5 %all-gather.5.cloned.1.call-start = ((), (), s32[]{:S(2)}) async-start(), calls=%async_computation.5 | async-start | bytes 3538944 | tf_op jit(solution)/shard_map/all_gather | solution.py:468
  286.6 10.9 %copy-start.6 = (bf16[512,3584]{1,0:T(8,128)(2,1)S(1)}, bf16[512,3584]{1,0:T(8,128)(2,1)}, u32[]{:S(2)}) copy-start(bf16[512,3584]{1,0:T(8,128)(2,1)} %get-tuple-element.9) | copy-start | bytes 11010052
  286.6 10.9 %copy-start.8 = (bf16[512,2304]{1,0:T(8,128)(2,1)S(1)}, bf16[512,2304]{1,0:T(8,128)(2,1)}, u32[]{:S(2)}) copy-start(bf16[512,2304]{1,0:T(8,128)(2,1)} %all-gather.5.cloned.1.call-done) | copy-start | bytes 7077892
  297.5 7.2 %copy-start.1 = (f32[512]{0:T(512)S(1)}, f32[512]{0:T(512)}, u32[]{:S(2)}) copy-start(f32[512]{0:T(512)} %param.27) | copy-start | bytes 6148
Sparse Core Ops, SparseCore 0:
  98.2 16.4 reduce-scatter.2
  118.9 12.2 all-gather.2
  263.2 7.4 reduce-scatter.4
  274.3 12.2 all-gather.4
